TPU v7x, 256 devices: a whole 4x4x8 slice. The times are simulated.
256 devices in a mesh: pages: 64 (over y, z, core), expert: 4 (over x).
Axes of the slice: x: 4, y: 4, z: 8, core: 2. Of those that a mesh axis runs over, the one named last changes fastest.
Arguments:
- old_keys: bfloat16 [512, 128, 2048], P('pages', None, 'expert'), may hold values from -6 to 6
- old_values: bfloat16 [512, 128, 2048], P('pages', None, 'expert'), may hold values from -6 to 6
- keep_lists: int32 [512, 31], P('pages'), may hold values from 0 to 127, as said below
- drop_weights: int32 [512, 128], P('pages'), may hold values from 1 to 8
- request_pages: int32 [64], replicated, may hold values from 4 to 12, as said below
- page_table: int32 [64, 12], replicated, may hold values from 0 to 511, as said below
- new_table: int32 [64, 3], replicated, may hold values from 0 to 255, as said below
- queries: bfloat16 [64, 2, 2048], P(None, None, 'expert'), may hold values from -20 to 20
- new_keys: bfloat16 [64, 2048], P('pages', 'expert'), may hold values from -12 to 12
- new_values: bfloat16 [64, 2048], P('pages', 'expert'), may hold values from -6 to 6
- expert_ids: int32 [64, 2], replicated, may hold values from 0 to 7, all different within a row
- router_logits: float32 [64, 8], P('pages'), may hold values from -6 to 6
- out_weight: bfloat16 [64, 2048, 256], P('pages', 'expert'), may hold values from -0.375 to 0.375
Outputs:
- compact_keys: bfloat16 [256, 128, 2048], P('pages', None, 'expert')
- compact_values: bfloat16 [256, 128, 2048], P('pages', None, 'expert')
- mixed: bfloat16 [64, 2048], P('pages', 'expert')
Inputs may be any that keep to these rules, and one draw needn't show every extreme that they name: `request_pages`: every count is a multiple of 4; the counts sum to 512; one request has 12 pages. `page_table`: the first request_pages[r] entries of row r name that request's old pages in order and later entries are unused; every old page belongs to exactly one request; old page g lies on index g // 8 of pages; no index of pages holds more than 1 old pages whose new pages lie on one index, and some index holds that many. `new_table`: the first request_pages[r] / 4 entries of row r name distinct new slots and later entries are unused; slot s lies on index s // 4 of pages; some index has all 4 of its slots used. `keep_lists`: each row holds 31 distinct positions in increasing order.
All inputs are finite; a program needn't handle non-finite values.
Results may differ from a plain program's by a relative error of at most 0.012.
Values may be sent and summed in bfloat16 or wider, within the bound.
No kernel may reach another device: no remote copies, remote signals or barrier semaphores. Data moves between devices by JAX's collectives and lax.ppermute only.
A program may use at most 64 MiB of HBM per device.

v0:
```python
import math
import jax
import jax.numpy as jnp
from jax import lax
from jax.sharding import PartitionSpec as P

HD = 128
EXPERTS = 8
NEGATIVE = -1e30


def compact_blocks(page_cache, pick_matrix, merge_coef, merge_total):
    kept_rows = jnp.einsum(
        "skt,stc->skc", pick_matrix, page_cache, preferred_element_type=jnp.float32
    )
    merged = (
        jnp.einsum("st,stc->sc", merge_coef, page_cache, preferred_element_type=jnp.float32)
        / merge_total[:, None]
    )
    return jnp.concatenate([kept_rows, merged[:, None, :]], axis=1).astype(jnp.bfloat16)


def local_scores(key_groups, group_req, group_live, queries, bias_row):
    groups, group_len, lane_width = key_groups.shape
    requests = queries.shape[0]
    topk_slots = queries.shape[1]
    head_count = lane_width // HD
    request_ids = jnp.arange(requests, dtype=jnp.int32)
    selected = (group_req[:, None] == request_ids[None, :]) & group_live[:, None]
    group_query = jnp.einsum(
        "gr,rkc->gkc", selected.astype(jnp.bfloat16), queries, preferred_element_type=jnp.float32
    ).astype(jnp.bfloat16)
    scores = jnp.einsum(
        "gkhd,glhd->gkhl",
        group_query.reshape(groups, topk_slots, head_count, HD),
        key_groups.reshape(groups, group_len, head_count, HD),
        preferred_element_type=jnp.float32,
    )
    scores = scores * (1.0 / math.sqrt(HD)) + bias_row[None, None, None, :]
    group_peak = jnp.max(scores, axis=3)
    request_peak = jnp.max(
        jnp.where(selected[:, :, None, None], group_peak[:, None, :, :], NEGATIVE), axis=0
    )
    return (selected, scores, request_peak)


def local_sums(selected, scores, value_groups, global_peak, group_live):
    groups, group_len, lane_width = value_groups.shape
    head_count = lane_width // HD
    topk_slots = scores.shape[1]
    highest = lax.Precision.HIGHEST
    chosen = selected.astype(jnp.float32)
    group_peak = jnp.einsum("gr,rkh->gkh", chosen, global_peak, precision=highest)
    terms = (
        jnp.exp(scores - group_peak[:, :, :, None])
        * group_live.astype(jnp.float32)[:, None, None, None]
    )
    numerator = jnp.einsum(
        "gkhl,glhd->gkhd",
        terms.astype(jnp.bfloat16),
        value_groups.reshape(groups, group_len, head_count, HD),
        preferred_element_type=jnp.float32,
    )
    numerator = numerator.reshape(groups, topk_slots, lane_width)
    request_num = jnp.einsum("gr,gkc->rkc", chosen, numerator, precision=highest)
    request_den = jnp.einsum("gr,gkh->rkh", chosen, jnp.sum(terms, axis=3), precision=highest)
    return (request_num, request_den)


def shards(
    old_keys,
    old_values,
    keep_lists,
    drop_weights,
    request_pages,
    page_table,
    new_table,
    queries,
    new_keys,
    new_values,
    expert_ids,
    router_logits,
    out_weight,
):
    devices = lax.axis_size("pages")
    shard_count = lax.axis_size("expert")
    my_index = lax.axis_index("pages")
    slots, page_len, lane_width = old_keys.shape
    keep_count = keep_lists.shape[1]
    block_rows = keep_count + 1
    per_new = page_len // block_rows
    requests, max_pages = page_table.shape
    max_new = new_table.shape[1]
    new_cap = 2 * (slots // per_new)
    capacity = (2 * slots + devices - 1) // devices
    head_count = lane_width // HD
    request_ids = jnp.arange(requests, dtype=jnp.int32)
    positions = jnp.arange(page_len, dtype=jnp.int32)
    picked = keep_lists[:, :, None] == positions[None, None, :]
    pick_matrix = picked.astype(jnp.bfloat16)
    merge_coef = jnp.where(jnp.any(picked, axis=1), 0.0, drop_weights.astype(jnp.float32))
    merge_total = jnp.sum(merge_coef, axis=1)
    key_blocks = compact_blocks(old_keys, pick_matrix, merge_coef.astype(jnp.bfloat16), merge_total)
    value_blocks = compact_blocks(
        old_values, pick_matrix, merge_coef.astype(jnp.bfloat16), merge_total
    )
    slot_ids = my_index * slots + jnp.arange(slots, dtype=jnp.int32)
    logical = jnp.arange(max_pages, dtype=jnp.int32)
    in_use = logical[None, :] < request_pages[:, None]
    found_at = (page_table[None, :, :] == slot_ids[:, None, None]) & in_use[None, :, :]
    owner_req = jnp.sum(jnp.where(found_at, request_ids[None, :, None], 0), axis=(1, 2))
    page_pos = jnp.sum(jnp.where(found_at, logical[None, None, :], 0), axis=(1, 2))
    fresh_slot = new_table[owner_req, page_pos // per_new]
    target_dev = fresh_slot // new_cap
    target_row = fresh_slot % new_cap * per_new + page_pos % per_new
    slot_order = jnp.arange(slots, dtype=jnp.int32)
    earlier = (target_dev[:, None] == target_dev[None, :]) & (
        slot_order[None, :] < slot_order[:, None]
    )
    send_pos = target_dev * capacity + jnp.sum(earlier, axis=1)
    outbox = send_pos[None, :] == jnp.arange(devices * capacity, dtype=jnp.int32)[:, None]
    outbox_matrix = outbox.astype(jnp.bfloat16)
    send_rows = (jnp.sum(jnp.where(outbox, target_row[None, :] + 1, 0), axis=1) - 1).reshape(
        devices, capacity
    )

    def pack_blocks(blocks):
        packed = jnp.einsum(
            "ps,sec->pec", outbox_matrix, blocks, preferred_element_type=jnp.float32
        )
        return packed.astype(jnp.bfloat16).reshape(devices, capacity, block_rows, lane_width)

    got_keys, got_values, got_rows = (
        lax.all_to_all(pack_blocks(key_blocks), "pages", split_axis=0, concat_axis=0, tiled=True),
        lax.all_to_all(pack_blocks(value_blocks), "pages", split_axis=0, concat_axis=0, tiled=True),
        lax.all_to_all(send_rows, "pages", split_axis=0, concat_axis=0, tiled=True),
    )
    landing = (
        got_rows.reshape(-1)[None, :] == jnp.arange(new_cap * per_new, dtype=jnp.int32)[:, None]
    ).astype(jnp.bfloat16)

    def land_blocks(received):
        flat_rows = received.reshape(devices * capacity, block_rows, lane_width)
        placed = jnp.einsum("qp,pec->qec", landing, flat_rows, preferred_element_type=jnp.float32)
        return placed.astype(jnp.bfloat16).reshape(new_cap, per_new * block_rows, lane_width)

    compact_keys = land_blocks(got_keys)
    compact_values = land_blocks(got_values)
    merge_bias = math.log(page_len - keep_count)
    bias_row = jnp.where(
        jnp.arange(per_new * block_rows) % block_rows == block_rows - 1, merge_bias, 0.0
    ).astype(jnp.float32)
    home_slots = my_index * new_cap + jnp.arange(new_cap, dtype=jnp.int32)
    new_live = jnp.arange(max_new, dtype=jnp.int32)[None, :] < (request_pages // per_new)[:, None]
    held_at = (new_table[None, :, :] == home_slots[:, None, None]) & new_live[None, :, :]
    group_req = jnp.sum(jnp.where(held_at, request_ids[None, :, None], 0), axis=(1, 2))
    group_live = jnp.any(held_at, axis=(1, 2))
    my_query = lax.dynamic_index_in_dim(queries, my_index, 0, keepdims=False)
    topk_slots = my_query.shape[0]
    own_score = jnp.einsum(
        "khd,hd->kh",
        my_query.reshape(topk_slots, head_count, HD),
        new_keys.reshape(head_count, HD),
        preferred_element_type=jnp.float32,
    ) * (1.0 / math.sqrt(HD))
    selected, scores, request_peak = local_scores(
        compact_keys, group_req, group_live, queries, bias_row
    )
    is_mine = (request_ids == my_index)[:, None, None]
    request_peak = jnp.where(
        is_mine, jnp.maximum(request_peak, own_score[None, :, :]), request_peak
    )
    global_peak = lax.pmax(request_peak, "pages")
    request_num, request_den = local_sums(selected, scores, compact_values, global_peak, group_live)
    my_num, my_den = (
        lax.psum_scatter(request_num, "pages", scatter_dimension=0, tiled=True),
        lax.psum_scatter(request_den, "pages", scatter_dimension=0, tiled=True),
    )
    my_peak = lax.dynamic_index_in_dim(global_peak, my_index, 0, keepdims=False)
    own_prob = jnp.exp(own_score - my_peak)
    own_rounded = lax.optimization_barrier(own_prob.astype(jnp.bfloat16)).astype(jnp.float32)
    numerator = (
        my_num[0].reshape(topk_slots, head_count, HD)
        + own_rounded[:, :, None]
        * new_values.reshape(head_count, HD).astype(jnp.float32)[None, :, :]
    )
    denominator = my_den[0] + own_prob
    my_experts = lax.dynamic_index_in_dim(expert_ids, my_index, 0, keepdims=False)
    chosen = jnp.take(router_logits[0], my_experts)
    gate_weights = jax.nn.softmax(chosen)
    weighted = (
        (gate_weights[:, None, None] * (numerator / denominator[:, :, None]))
        .astype(jnp.bfloat16)
        .reshape(1, topk_slots, lane_width)
    )
    column_blocks = devices // EXPERTS
    my_expert = my_index // column_blocks
    weight_block = out_weight[0]
    match_mask = (expert_ids == my_expert).astype(jnp.bfloat16)
    contrib = jnp.einsum(
        "rkc,rk,co->ro",
        lax.all_gather(weighted, "pages", axis=0, tiled=True),
        match_mask,
        weight_block,
        preferred_element_type=jnp.float32,
    )
    block_cols = contrib.shape[1]
    model_width = block_cols * column_blocks
    full_rows = jnp.zeros((requests, model_width), jnp.float32)
    full_rows = lax.dynamic_update_slice(
        full_rows, contrib, (jnp.zeros((), jnp.int32), my_index % column_blocks * block_cols)
    )
    spread = full_rows.reshape(requests * shard_count, model_width // shard_count)
    mixed = lax.psum_scatter(spread, ("pages", "expert"), scatter_dimension=0, tiled=True).astype(
        jnp.bfloat16
    )
    return (compact_keys, compact_values, mixed)


def solution(mesh):
    in_specs = (
        P("pages", None, "expert"),
        P("pages", None, "expert"),
        P("pages", None),
        P("pages", None),
        P(),
        P(),
        P(),
        P(None, None, "expert"),
        P("pages", "expert"),
        P("pages", "expert"),
        P(),
        P("pages", None),
        P("pages", "expert", None),
    )
    out_specs = (P("pages", None, "expert"), P("pages", None, "expert"), P("pages", "expert"))
    return jax.shard_map(shards, mesh=mesh, in_specs=in_specs, out_specs=out_specs, check_vma=False)
```

profile of v0, /device:TPU:1, one launch (start us, length us, event | category | flops | bytes accessed | tf_op | source)
XLA Modules:
  0.0 820.6 jit_solution(7523858380768102113)
XLA Ops:
  8.0 0.9 select_reduce_fusion.1
  9.0 1.3 gather_fusion
  11.3 13.2 %all-to-all-start = ((s32[64,1,1]{2,1,0:T(1,128)}), s32[64,1,1]{2,1,0:T(1,128)S(1)}, u32[]{:S(2)}, u32[]{:S(2)}) async-start(s32[64,1,1]{2,1,0:T(1,128)} %copy.104), calls=%async_computation | async-start | bytes 65536 | tf_op jit(solution)/shard_map/all_to_all | solution.py:136
  25.3 1.0 convolution_convert_fusion.1
  28.6 2.5 copy.107
  31.1 2.6 all-to-all-done
  33.7 7.8 all-to-all-start.1
  41.6 1.5 convolution_convert_fusion
  43.2 0.8 convert_bitcast_fusion
  44.0 2.5 copy.112
  46.6 46.2 %all-to-all-done.1 = bf16[64,1,32,512]{3,2,1,0:T(8,128)(2,1)S(1)} async-done(((bf16[64,1,32,512]{3,2,1,0:T(8,128)(2,1)}), bf16[64,1,32,512]{3,2,1,0:T(8,128)(2,1)S(1)}, u32[]{:S(2)}, u32[]{:S(2)}) %all-to-all-start.1) | async-done | bytes 2097184 | tf_op jit(solution)/shard_map/all_to_all | solution.py:134
  92.8 6.0 all-to-all-start.2
  102.2 1.2 fusion.77
  103.4 1.3 broadcast_divide_fusion
  104.7 1.2 reduce
  106.0 2.3 fusion.6
  109.5 153.3 %pmax.7 = f32[64,2,4]{0,2,1:T(4,128)S(1)} all-reduce(f32[64,2,4]{0,2,1:T(4,128)S(1)} %maximum_select_fusion), channel_id=1, replica_groups=mesh['pages'=64,'expert'=4] {'pages'}, use_global_device_ids=true, to_apply=%region_12.13 | all-reduce | flops 512 | bytes 4096 | tf_op jit(solution)/shard_map/pmax | solution.py:173
  263.0 4.0 fusion.9
  268.0 242.0 %all-reduce.1 = f32[64,2,4]{2,1,0:T(2,128)S(1)} all-reduce(f32[64,2,4]{2,1,0:T(2,128)S(1)} %copy.126), channel_id=3, replica_groups=mesh['pages'=64,'expert'=4] {'pages'}, use_global_device_ids=true, to_apply=%region_15.16.clone | all-reduce | flops 512 | bytes 4096
  510.9 0.9 copy.124
  512.6 173.4 %all-reduce.6.cloned.1.call-done = f32[64,2,512]{2,1,0:T(2,128)} async-done(((f32[64,2,512]{2,1,0:T(2,128)}), f32[64,2,512]{2,1,0:T(2,128)}) %all-reduce.6.cloned.1.call-update) | async-done | bytes 262160
  686.0 1.4 multiply_convert_fusion
  687.4 47.0 %all_gather.3 = bf16[64,2,512]{2,1,0:T(2,128)(2,1)S(1)} all-gather(bf16[1,2,512]{2,1,0:T(2,128)(2,1)S(1)} %multiply_convert_fusion), channel_id=1, replica_groups=mesh['pages'=64,'expert'=4] {'pages'}, dimensions={0}, use_global_device_ids=true | all-gather | bytes 133120 | tf_op jit(solution)/shard_map/all_gather | solution.py:202
  735.1 78.0 %all-reduce.7 = bf16[256,512]{1,0:T(8,128)(2,1)S(1)} all-reduce(f32[256,512]{1,0:T(8,128)S(1)} %reshape.410), channel_id=4, replica_groups=mesh['pages'=64,'expert'=4] {'pages','expert'}, use_global_device_ids=true, to_apply=%region_16.17.clone | all-reduce | flops 131072 | bytes 786432
  (100 shorter events, 13.6 us)
Async XLA Ops:
  7.2 18.1 %copy-start = (bf16[8,128,512]{2,1,0:T(8,128)(2,1)S(1)}, bf16[8,128,512]{2,1,0:T(8,128)(2,1)}, u32[]{:S(2)}) copy-start(bf16[8,128,512]{2,1,0:T(8,128)(2,1)} %param.13) | copy-start | bytes 3145732
  7.2 20.2 %copy-start.3 = (bf16[8,128,512]{2,1,0:T(8,128)(2,1)S(1)}, bf16[8,128,512]{2,1,0:T(8,128)(2,1)}, u32[]{:S(2)}) copy-start(bf16[8,128,512]{2,1,0:T(8,128)(2,1)} %param.14) | copy-start | bytes 3145732
  11.3 22.4 %all-to-all-start = ((s32[64,1,1]{2,1,0:T(1,128)}), s32[64,1,1]{2,1,0:T(1,128)S(1)}, u32[]{:S(2)}, u32[]{:S(2)}) async-start(s32[64,1,1]{2,1,0:T(1,128)} %copy.104), calls=%async_computation | async-start | bytes 65536 | tf_op jit(solution)/shard_map/all_to_all | solution.py:136
  31.1 10.5 %copy-start.8 = (s32[8,31]{1,0:T(8,128)S(1)}, s32[8,31]{1,0:T(8,128)}, u32[]{:S(2)}) copy-start(s32[8,31]{1,0:T(8,128)} %param.15) | copy-start | bytes 2980
  33.7 59.1 %all-to-all-start.1 = ((bf16[64,1,32,512]{3,2,1,0:T(8,128)(2,1)}), bf16[64,1,32,512]{3,2,1,0:T(8,128)(2,1)S(1)}, u32[]{:S(2)}, u32[]{:S(2)}) async-start(bf16[64,1,32,512]{3,2,1,0:T(8,128)(2,1)} %copy.107), calls=%async_computation.1 | async-start | bytes 4194304 | tf_op jit(solution)/shard_map/all_to_all | solution.py:134
  46.5 52.5 %copy-start.11 = (s32[64]{0:T(128)S(1)}, s32[64]{0:T(128)}, u32[]{:S(2)}) copy-start(s32[64]{0:T(128)} %param.17) | copy-start | bytes 772
  46.5 52.6 %copy-start.2 = (s32[64,3]{0,1:T(4,128)S(1)}, s32[64,3]{0,1:T(4,128)}, u32[]{:S(2)}) copy-start(s32[64,3]{0,1:T(4,128)} %param.19) | copy-start | bytes 2308
  46.5 53.0 %copy-start.7 = (bf16[64,2,512]{2,1,0:T(2,128)(2,1)S(1)}, bf16[64,2,512]{2,1,0:T(2,128)(2,1)}, u32[]{:S(2)}) copy-start(bf16[64,2,512]{2,1,0:T(2,128)(2,1)} %param.20) | copy-start | bytes 393220
  46.5 53.2 %copy-start.12 = (bf16[1,512]{1,0:T(2,128)(2,1)S(1)}, bf16[1,512]{1,0:T(2,128)(2,1)}, u32[]{:S(2)}) copy-start(bf16[1,512]{1,0:T(2,128)(2,1)} %param.21) | copy-start | bytes 3076
  46.5 53.4 %copy-start.9 = (s32[64,2]{0,1:T(2,128)S(1)}, s32[64,2]{0,1:T(2,128)}, u32[]{:S(2)}) copy-start(s32[64,2]{0,1:T(2,128)} %param.23) | copy-start | bytes 1540
  46.5 53.6 %copy-start.10 = (bf16[1,512]{1,0:T(2,128)(2,1)S(1)}, bf16[1,512]{1,0:T(2,128)(2,1)}, u32[]{:S(2)}) copy-start(bf16[1,512]{1,0:T(2,128)(2,1)} %param.22) | copy-start | bytes 3076
  46.5 53.8 %copy-start.13 = (u32[256]{0:T(256)S(1)}, u32[256]{0:T(256)}, u32[]{:S(2)}) copy-start(u32[256]{0:T(256)} %constant.168) | copy-start | bytes 3076
  46.6 54.4 %copy-start.1 = (f32[1,8]{1,0:T(1,128)S(1)}, f32[1,8]{1,0:T(1,128)}, u32[]{:S(2)}) copy-start(f32[1,8]{1,0:T(1,128)} %param.24) | copy-start | bytes 100
  92.8 170.3 %all-to-all-start.2 = ((bf16[64,1,32,512]{3,2,1,0:T(8,128)(2,1)}), bf16[64,1,32,512]{3,2,1,0:T(8,128)(2,1)}, u32[]{:S(2)}, u32[]{:S(2)}) async-start(bf16[64,1,32,512]{3,2,1,0:T(8,128)(2,1)} %copy.112), calls=%async_computation.2 | async-start | bytes 4194304 | tf_op jit(solution)/shard_map/all_to_all | solution.py:135
  98.8 587.3 %all-reduce.6.cloned.1.call-start = ((), (), s32[]{:S(2)}) async-start(), calls=%async_computation.3 | async-start | bytes 524288
  108.6 158.4 %copy-start.4 = (bf16[16,32,512]{2,1,0:T(8,128)(2,1)}, bf16[16,32,512]{2,1,0:T(8,128)(2,1)S(1)}, u32[]{:S(2)}) copy-start(bf16[16,32,512]{2,1,0:T(8,128)(2,1)S(1)} %copy.109) | copy-start | bytes 1572868
  267.3 467.5 %copy-start.5 = (bf16[16,32,512]{2,1,0:T(8,128)(2,1)}, bf16[16,32,512]{2,1,0:T(8,128)(2,1)S(1)}, u32[]{:S(2)}) copy-start(bf16[16,32,512]{2,1,0:T(8,128)(2,1)S(1)} %copy.114) | copy-start | bytes 1572868
  510.1 224.7 %copy-start.6 = (bf16[1,512,256]{2,1,0:T(8,128)(2,1)S(1)}, bf16[1,512,256]{2,1,0:T(8,128)(2,1)}, u32[]{:S(2)}) copy-start(bf16[1,512,256]{2,1,0:T(8,128)(2,1)} %param.25) | copy-start | bytes 786436
Sparse Core Ops, SparseCore 0:
  511.9 174.0 all-reduce.5
where the time goes:
time: 821 us
  blocking collectives  520 us (63%)
  waiting for transfers between devices  222 us (27%)
  starting transfers between devices  27.2 us (3%)
  between operations  14.5 us (2%)
  matrix products  13.1 us (2%)
  local copies, waits for them, and re-layouts  12 us (1%)
  other arithmetic  11.1 us (1%)
    unnamed x2, blocking collectives  320 us
    unnamed x2, waiting for transfers between devices  173 us
    pmax x1, blocking collectives, shards(): global_peak = lax.pmax(request_peak, 'pages')  153 us
    all_gather x1, blocking collectives, shards(): lax.all_gather(weighted, 'pages', axis=0, tiled=True)  47 us
    all_to_all x1, waiting for transfers between devices, shards(): lax.all_to_all(pack_blocks(key_blocks), 'pages', split_axis=0, concat_axi...  46.2 us
  transfers between devices with their start and end apart: 4, of which 3 were waited for; matrix products, arithmetic and copies ran while one was open for 3% of the time, Pallas kernels for 0%

commit v1 on v0

--- a/solution.py
+++ b/solution.py
@@ -7,6 +7,9 @@
 HD = 128
 EXPERTS = 8
 NEGATIVE = -1e30
+finish_the_shards = lambda state, comm_axis, d0: jnp.concatenate(
+    lax.all_to_all(jnp.stack([state for _ in range(lax.axis_size(comm_axis))]), comm_axis, 0, 0), d0
+)
 
 
 def compact_blocks(page_cache, pick_matrix, merge_coef, merge_total):
@@ -199,7 +202,7 @@
     match_mask = (expert_ids == my_expert).astype(jnp.bfloat16)
     contrib = jnp.einsum(
         "rkc,rk,co->ro",
-        lax.all_gather(weighted, "pages", axis=0, tiled=True),
+        finish_the_shards(weighted, "pages", 0),
         match_mask,
         weight_block,
         preferred_element_type=jnp.float32,

time: 821 us -> 791 us (0.963)
  blocking collectives: 520 us -> 468 us
  waiting for transfers between devices: 222 us -> 232 us
    all_gather x1 -> x0, blocking collectives: 47 us -> none  [shards(): lax.all_gather(weighted, 'pages', axis=0, tiled=True)]
    all_to_all x0 -> x1, waiting for transfers between devices: none -> 10.2 us  [lax.all_to_all(jnp.stack([state for _ in range(lax.axis_size(comm_axis))]...]
  transfers between devices with their start and end apart: 4 -> 5, of which waited for: 3 -> 4; matrix products, arithmetic and copies ran while one was open for 3% -> 4% of each run, Pallas kernels for 0% -> 0%
where the time goes in v1:
time: 791 us; the launch traced here: 790 us
  blocking collectives  468 us (59%)
  waiting for transfers between devices  232 us (29%)
  starting transfers between devices  33.6 us (4%)
  local copies, waits for them, and re-layouts  16.7 us (2%)
  between operations  14.5 us (2%)
  matrix products  14.2 us (2%)
  other arithmetic  11.1 us (1%)
    unnamed x2, blocking collectives  320 us
    unnamed x2, waiting for transfers between devices  173 us
    pmax x1, blocking collectives, shards(): global_peak = lax.pmax(request_peak, 'pages')  148 us
    all_to_all x1, waiting for transfers between devices, shards(): lax.all_to_all(pack_blocks(key_blocks), 'pages', split_axis=0, concat_axi...  46.2 us
  transfers between devices with their start and end apart: 5, of which 4 were waited for; matrix products, arithmetic and copies ran while one was open for 4% of the time, Pallas kernels for 0%

profile of v1, /device:TPU:1, one launch (start us, length us, event | category | flops | bytes accessed | tf_op | source)
XLA Modules:
  0.0 790.4 jit_solution(7876076398869709167)
XLA Ops:
  9.0 1.3 gather_fusion
  11.3 13.2 %all-to-all-start = ((s32[64,1,1]{2,1,0:T(1,128)}), s32[64,1,1]{2,1,0:T(1,128)S(1)}, u32[]{:S(2)}, u32[]{:S(2)}) async-start(s32[64,1,1]{2,1,0:T(1,128)} %copy.106), calls=%async_computation | async-start | bytes 65536 | tf_op jit(solution)/shard_map/all_to_all | solution.py:139
  28.6 2.5 copy.109
  31.1 2.6 all-to-all-done
  33.7 7.8 all-to-all-start.1
  41.6 1.5 convolution_convert_fusion
  44.0 2.5 copy.114
  46.6 46.2 %all-to-all-done.1 = bf16[64,1,32,512]{3,2,1,0:T(8,128)(2,1)S(1)} async-done(((bf16[64,1,32,512]{3,2,1,0:T(8,128)(2,1)}), bf16[64,1,32,512]{3,2,1,0:T(8,128)(2,1)S(1)}, u32[]{:S(2)}, u32[]{:S(2)}) %all-to-all-start.1) | async-done | bytes 2097184 | tf_op jit(solution)/shard_map/all_to_all | solution.py:137
  92.8 1.3 copy-done.3
  94.1 5.8 all-to-all-start.2
  103.1 1.2 fusion.80
  104.4 1.3 broadcast_divide_fusion
  105.7 1.2 reduce
  106.9 3.9 fusion.6
  111.9 2.0 reshape_reshape.7
  113.9 1.5 fusion.83
  115.6 148.4 %pmax.7 = f32[64,2,4]{0,2,1:T(4,128)S(1)} all-reduce(f32[64,2,4]{0,2,1:T(4,128)S(1)} %maximum_select_fusion), channel_id=1, replica_groups=mesh['pages'=64,'expert'=4] {'pages'}, use_global_device_ids=true, to_apply=%region_12.13 | all-reduce | flops 512 | bytes 4096 | tf_op jit(solution)/shard_map/pmax | solution.py:176
  264.3 2.4 fusion.9
  267.7 242.0 %all-reduce.1 = f32[64,2,4]{2,1,0:T(2,128)S(1)} all-reduce(f32[64,2,4]{2,1,0:T(2,128)S(1)} %copy.128), channel_id=3, replica_groups=mesh['pages'=64,'expert'=4] {'pages'}, use_global_device_ids=true, to_apply=%region_15.16.clone | all-reduce | flops 512 | bytes 4096
  512.3 173.4 %all-reduce.6.cloned.1.call-done = f32[64,2,512]{2,1,0:T(2,128)} async-done(((f32[64,2,512]{2,1,0:T(2,128)}), f32[64,2,512]{2,1,0:T(2,128)}) %all-reduce.6.cloned.1.call-update) | async-done | bytes 262160
  685.6 1.4 fusion.64
  687.8 6.6 all-to-all-start.3
  694.5 10.2 %all-to-all-done.3 = bf16[64,1,2,512]{3,2,1,0:T(2,128)(2,1)S(1)} async-done(((bf16[64,1,2,512]{3,2,1,0:T(2,128)(2,1)}), bf16[64,1,2,512]{3,2,1,0:T(2,128)(2,1)S(1)}, u32[]{:S(2)}, u32[]{:S(2)}) %all-to-all-start.3) | async-done | bytes 131104 | tf_op jit(solution)/shard_map/all_to_all | solution.py:11
  705.4 77.6 %all-reduce.7 = bf16[256,512]{1,0:T(8,128)(2,1)S(1)} all-reduce(f32[256,512]{1,0:T(8,128)S(1)} %reshape.416), channel_id=4, replica_groups=mesh['pages'=64,'expert'=4] {'pages','expert'}, use_global_device_ids=true, to_apply=%region_16.17.clone | all-reduce | flops 131072 | bytes 786432
  (102 shorter events, 18.1 us)
Async XLA Ops:
  7.2 18.1 %copy-start = (bf16[8,128,512]{2,1,0:T(8,128)(2,1)S(1)}, bf16[8,128,512]{2,1,0:T(8,128)(2,1)}, u32[]{:S(2)}) copy-start(bf16[8,128,512]{2,1,0:T(8,128)(2,1)} %param.13) | copy-start | bytes 3145732
  7.2 20.2 %copy-start.4 = (bf16[8,128,512]{2,1,0:T(8,128)(2,1)S(1)}, bf16[8,128,512]{2,1,0:T(8,128)(2,1)}, u32[]{:S(2)}) copy-start(bf16[8,128,512]{2,1,0:T(8,128)(2,1)} %param.14) | copy-start | bytes 3145732
  11.3 22.4 %all-to-all-start = ((s32[64,1,1]{2,1,0:T(1,128)}), s32[64,1,1]{2,1,0:T(1,128)S(1)}, u32[]{:S(2)}, u32[]{:S(2)}) async-start(s32[64,1,1]{2,1,0:T(1,128)} %copy.106), calls=%async_computation | async-start | bytes 65536 | tf_op jit(solution)/shard_map/all_to_all | solution.py:139
  31.1 10.5 %copy-start.8 = (s32[8,31]{1,0:T(8,128)S(1)}, s32[8,31]{1,0:T(8,128)}, u32[]{:S(2)}) copy-start(s32[8,31]{1,0:T(8,128)} %param.15) | copy-start | bytes 2980
  33.7 59.1 %all-to-all-start.1 = ((bf16[64,1,32,512]{3,2,1,0:T(8,128)(2,1)}), bf16[64,1,32,512]{3,2,1,0:T(8,128)(2,1)S(1)}, u32[]{:S(2)}, u32[]{:S(2)}) async-start(bf16[64,1,32,512]{3,2,1,0:T(8,128)(2,1)} %copy.109), calls=%async_computation.1 | async-start | bytes 4194304 | tf_op jit(solution)/shard_map/all_to_all | solution.py:137
  46.5 53.7 %copy-start.11 = (s32[64]{0:T(128)S(1)}, s32[64]{0:T(128)}, u32[]{:S(2)}) copy-start(s32[64]{0:T(128)} %param.17) | copy-start | bytes 772
  46.5 53.7 %copy-start.2 = (s32[64,3]{0,1:T(4,128)S(1)}, s32[64,3]{0,1:T(4,128)}, u32[]{:S(2)}) copy-start(s32[64,3]{0,1:T(4,128)} %param.19) | copy-start | bytes 2308
  46.5 54.2 %copy-start.7 = (bf16[64,2,512]{2,1,0:T(2,128)(2,1)S(1)}, bf16[64,2,512]{2,1,0:T(2,128)(2,1)}, u32[]{:S(2)}) copy-start(bf16[64,2,512]{2,1,0:T(2,128)(2,1)} %param.20) | copy-start | bytes 393220
  46.5 54.3 %copy-start.12 = (bf16[1,512]{1,0:T(2,128)(2,1)S(1)}, bf16[1,512]{1,0:T(2,128)(2,1)}, u32[]{:S(2)}) copy-start(bf16[1,512]{1,0:T(2,128)(2,1)} %param.21) | copy-start | bytes 3076
  46.5 54.5 %copy-start.10 = (bf16[1,512]{1,0:T(2,128)(2,1)S(1)}, bf16[1,512]{1,0:T(2,128)(2,1)}, u32[]{:S(2)}) copy-start(bf16[1,512]{1,0:T(2,128)(2,1)} %param.22) | copy-start | bytes 3076
  46.5 54.5 %copy-start.9 = (s32[64,2]{0,1:T(2,128)S(1)}, s32[64,2]{0,1:T(2,128)}, u32[]{:S(2)}) copy-start(s32[64,2]{0,1:T(2,128)} %param.23) | copy-start | bytes 1540
  46.5 54.7 %copy-start.13 = (u32[256]{0:T(256)S(1)}, u32[256]{0:T(256)}, u32[]{:S(2)}) copy-start(u32[256]{0:T(256)} %constant.168) | copy-start | bytes 3076
  46.5 55.3 %copy-start.1 = (f32[1,8]{1,0:T(1,128)S(1)}, f32[1,8]{1,0:T(1,128)}, u32[]{:S(2)}) copy-start(f32[1,8]{1,0:T(1,128)} %param.24) | copy-start | bytes 100
  92.8 1.3 copy-start.3
  94.1 170.3 %all-to-all-start.2 = ((bf16[64,1,32,512]{3,2,1,0:T(8,128)(2,1)}), bf16[64,1,32,512]{3,2,1,0:T(8,128)(2,1)S(1)}, u32[]{:S(2)}, u32[]{:S(2)}) async-start(bf16[64,1,32,512]{3,2,1,0:T(8,128)(2,1)} %copy.114), calls=%async_computation.2 | async-start | bytes 4194304 | tf_op jit(solution)/shard_map/all_to_all | solution.py:138
  99.9 585.8 %all-reduce.6.cloned.1.call-start = ((), (), s32[]{:S(2)}) async-start(), calls=%async_computation.4 | async-start | bytes 524288
  267.0 438.0 %copy-start.5 = (bf16[16,32,512]{2,1,0:T(8,128)(2,1)}, bf16[16,32,512]{2,1,0:T(8,128)(2,1)S(1)}, u32[]{:S(2)}) copy-start(bf16[16,32,512]{2,1,0:T(8,128)(2,1)S(1)} %copy.116) | copy-start | bytes 1572868
  509.8 195.2 %copy-start.6 = (bf16[1,512,256]{2,1,0:T(8,128)(2,1)S(1)}, bf16[1,512,256]{2,1,0:T(8,128)(2,1)}, u32[]{:S(2)}) copy-start(bf16[1,512,256]{2,1,0:T(8,128)(2,1)} %param.25) | copy-start | bytes 786436
  687.8 16.9 %all-to-all-start.3 = ((bf16[64,1,2,512]{3,2,1,0:T(2,128)(2,1)}), bf16[64,1,2,512]{3,2,1,0:T(2,128)(2,1)S(1)}, u32[]{:S(2)}, u32[]{:S(2)}) async-start(bf16[64,1,2,512]{3,2,1,0:T(2,128)(2,1)} %stack.3), calls=%async_computation.3 | async-start | bytes 262144 | tf_op jit(solution)/shard_map/all_to_all | solution.py:11
Sparse Core Ops, SparseCore 0:
  511.5 174.0 all-reduce.5
